TPU v7x, 32 devices: a whole 2x2x4 slice. The times are simulated.
32 devices in a mesh: fsdp: 16 (over z, x, core), dp: 2 (over y).
Axes of the slice: x: 2, y: 2, z: 4, core: 2. Of those that a mesh axis runs over, the one named last changes fastest.
Arguments:
- tokens: bfloat16 [32768, 768], P(('fsdp', 'dp')), may hold values from -6 to 6
- segment_ids: int32 [32, 1024], P(('fsdp', 'dp')), may hold values from -1 to 15, as said below
- projection: float32 [12, 32, 64], replicated, may hold values from -0.75 to 0.75
- norm1_gain: bfloat16 [768], P('fsdp'), may hold values from 0.5 to 1.5
- norm1_bias: bfloat16 [768], P('fsdp'), may hold values from -1.1953125 to 1.1953125
- qkv_weight: bfloat16 [768, 2304], P('fsdp'), may hold values from -0.21875 to 0.21875
- qkv_bias: bfloat16 [2304], P('fsdp'), may hold values from -1.1953125 to 1.1953125
- out_weight: bfloat16 [768, 768], P('fsdp'), may hold values from -1.5 to 1.5
- out_bias: bfloat16 [768], P('fsdp'), may hold values from -1.1953125 to 1.1953125
- norm2_gain: bfloat16 [768], P('fsdp'), may hold values from 0.5 to 1.5
- norm2_bias: bfloat16 [768], P('fsdp'), may hold values from -1.1953125 to 1.1953125
- in_weight: bfloat16 [768, 3072], P('fsdp'), may hold values from -0.21875 to 0.21875
- in_bias: bfloat16 [3072], P('fsdp'), may hold values from -1.1953125 to 1.1953125
- ffn_out_weight: bfloat16 [3072, 768], P('fsdp'), may hold values from -0.109375 to 0.109375
- ffn_out_bias: bfloat16 [768], P('fsdp'), may hold values from -1.1953125 to 1.1953125
- cotangent: bfloat16 [32768, 768], P(('fsdp', 'dp')), may hold values from -6 to 6
Outputs:
- output: bfloat16 [32768, 768], P(('fsdp', 'dp'))
- tokens_grad: bfloat16 [32768, 768], P(('fsdp', 'dp'))
- norm1_gain_grad: float32 [768], P('fsdp')
- norm1_bias_grad: float32 [768], P('fsdp')
- qkv_weight_grad: float32 [768, 2304], P('fsdp')
- query_key_bias_grad: float32 [1536], P('fsdp')
- value_bias_grad: float32 [768], P('fsdp')
- out_weight_grad: float32 [768, 768], P('fsdp')
- out_bias_grad: float32 [768], P('fsdp')
- norm2_gain_grad: float32 [768], P('fsdp')
- norm2_bias_grad: float32 [768], P('fsdp')
- in_weight_grad: float32 [768, 3072], P('fsdp')
- in_bias_grad: float32 [3072], P('fsdp')
- ffn_out_weight_grad: float32 [3072, 768], P('fsdp')
- ffn_out_bias_grad: float32 [768], P('fsdp')
Inputs may be any that keep to these rules, and one draw needn't show every extreme that they name: `segment_ids`: in each sequence the ids never fall until the padding; the last 1 to 256 rows of every sequence are -1 and no others; every sequence reaches id 16 - 1; some segments may have no rows.
All inputs are finite; a program needn't handle non-finite values.
Results may differ from a plain program's by a relative error of at most 0.01.
Values may be sent and summed in bfloat16 or wider, within the bound.
A program may use at most 192 MiB of HBM per device.

v0:
```python
import functools

import jax
import jax.numpy as jnp
import numpy as np
from jax import lax
from jax.experimental import pallas as pl
from jax.experimental.pallas import tpu as pltpu
from jax.sharding import PartitionSpec as P

HEADS = 12
HEAD_DIM = 64
FEATS = 32
SEGS = 16
PACK = 4
GROUPS = HEADS // PACK
WIDE = PACK * HEAD_DIM
SLIM = PACK * FEATS
STATE = SEGS * SLIM
EPSILON = 1e-05
F32 = jnp.float32
BF16 = jnp.bfloat16
VMEM_LIMIT = 67_000_000

GAIN1, SHIFT1, BIAS_OUT, GAIN2, SHIFT2, BIAS_FFO, BIAS_QKV, BIAS_IN = range(8)
QUERY_KEY, VALUE = 8, 9


def contract(left, right, left_dim, right_dim):
    return lax.dot_general(
        left, right, (((left_dim,), (right_dim,)), ((), ())), preferred_element_type=F32
    )


def nn(left, right):
    return contract(left, right, 1, 0)


def nt(left, right):
    return contract(left, right, 1, 1)


def tn(left, right):
    return contract(left, right, 0, 0)


def tile(index, size):
    return pl.ds(pl.multiple_of(index * size, size), size)


def iota(shape, dim):
    return lax.broadcasted_iota(jnp.int32, shape, dim)


def split_two(values):
    high = values.astype(BF16)
    return high, (values - high.astype(F32)).astype(BF16)


def normalize(rows):
    centred = rows - jnp.mean(rows, axis=-1, keepdims=True)
    inv_std = lax.rsqrt(jnp.mean(centred * centred, axis=-1, keepdims=True) + EPSILON)
    return centred * inv_std, inv_std


def normalize_back(incoming, normed, inv_std, gain):
    scaled = incoming * gain
    mean_one = jnp.mean(scaled, axis=-1, keepdims=True)
    mean_two = jnp.mean(scaled * normed, axis=-1, keepdims=True)
    return inv_std * (scaled - mean_one - normed * mean_two)


def column_sum(values):
    return jnp.sum(values, axis=0, keepdims=True)


def head_blocks(rows, columns, row_width, column_width):
    return (iota((rows, columns), 0) // row_width) == (iota((rows, columns), 1) // column_width)


def ones_where(mask):
    return jnp.where(mask, 1.0, 0.0).astype(BF16)


def projection_blocks(proj_ref, group):
    small = proj_ref[tile(group, SLIM), :].astype(BF16)
    source, lane = iota((HEAD_DIM, WIDE), 0), iota((HEAD_DIM, WIDE), 1) % HEAD_DIM
    half = HEAD_DIM // 2
    plain = jnp.where(source == lane, 1.0, 0.0)
    turned = jnp.where(source == (lane + half) % HEAD_DIM, jnp.where(lane < half, 1.0, -1.0), 0.0)
    keep = head_blocks(SLIM, WIDE, FEATS, HEAD_DIM)
    return (
        jnp.where(keep, nn(small, plain.astype(BF16)), 0.0).astype(BF16),
        jnp.where(keep, nn(small, turned.astype(BF16)), 0.0).astype(BF16),
    )


def segment_masks(seg_ref, one_ref, ids_ref):
    length = seg_ref.shape[1]
    one_ref[...] = ones_where(iota((SEGS, length), 0) == seg_ref[...])
    codes = (iota((SEGS, SLIM), 0) + 1).astype(F32).astype(BF16)

    @pl.loop(0, length // 256)
    def _(r):
        ids_ref[tile(r, 256), :] = tn(one_ref[:, tile(r, 256)], codes) - 1.0


def denominators(fq, one_rows, total):
    high, low = split_two(total)
    total_rows = tn(one_rows, high) + tn(one_rows, low)
    absent = 1.0 - tn(one_rows, jnp.ones((SEGS, WIDE), BF16))
    products = (fq.astype(F32) * total_rows).astype(BF16)
    wide = nn(products, ones_where(head_blocks(SLIM, WIDE, FEATS, HEAD_DIM))) + absent
    slim = nn(products, ones_where(head_blocks(SLIM, SLIM, FEATS, FEATS))) + absent[:, :SLIM]
    return total_rows, wide, slim, absent


def spread(features, ids):
    wide = features.astype(F32)
    return jnp.concatenate([jnp.where(ids == s, wide, 0.0).astype(BF16) for s in range(SEGS)], axis=1)


def segment_states(feature_ref, one_ref, value, group, out_ref, base):
    turned = feature_ref[:, tile(group, SLIM)].astype(F32).T.astype(BF16)
    keep = head_blocks(SLIM, WIDE, FEATS, HEAD_DIM)
    chunk = 8
    for part in range(SEGS // chunk):
        left = jnp.concatenate(
            [turned * one_ref[s : s + 1, :] for s in range(part * chunk, (part + 1) * chunk)], axis=0
        )
        sums = nn(left, value)
        for s in range(chunk):
            piece = jnp.where(keep, sums[s * SLIM : (s + 1) * SLIM], 0.0).astype(BF16)
            row = base + (part * chunk + s) * SLIM
            out_ref[pl.ds(pl.multiple_of(row, SLIM), SLIM), :] = piece


def masked_sum(products, ids):
    out = jnp.where(ids == 0, products[:, :SLIM], 0.0)
    for s in range(1, SEGS):
        out = out + jnp.where(ids == s, products[:, s * SLIM : (s + 1) * SLIM], 0.0)
    return out


def twice(table):
    return jnp.concatenate([table, table], axis=1)


class Poll:
    def __init__(self, *plan):
        self.plan = plan


def checkpoint(poll, index=0, stride=1, base=0, inner=0, count=1):
    if poll is None:
        return
    now = index * stride + base + inner
    for number, steps in enumerate(poll.plan):
        if not steps or not base <= number % stride < base + count:
            continue

        @pl.when(now == number)
        def _(steps=steps):
            for step in steps:
                step()


def phase_normalize(tok_ref, normed_ref):
    @pl.loop(0, tok_ref.shape[0] // 256)
    def _(r):
        normed_ref[tile(r, 256), :] = normalize(tok_ref[tile(r, 256), :].astype(F32))[0]


def phase_norm_one(normed_ref, vec_ref, h1_ref, hbar_ref):
    length, width = normed_ref.shape
    hbar_ref[...] = jnp.zeros_like(hbar_ref)

    @pl.loop(0, length // 256)
    def _(r):
        normed = normed_ref[tile(r, 256), :]
        rows = normed * vec_ref[GAIN1 : GAIN1 + 1, :width] + vec_ref[SHIFT1 : SHIFT1 + 1, :width]
        h1_ref[tile(r, 256), :] = rows.astype(BF16)
        hbar_ref[0:1, :] += column_sum(rows) * (1.0 / length)


def phase_attention(
    h1_ref, hbar_ref, w_qkv_ref, vec_ref, proj_ref, cos_ref, sin_ref, one_ref, ids_ref,
    fq_ref, fk_ref, sq_ref, sk_ref, v_ref, state_ref, total_ref, att_ref, attc_ref, poll=None,
):
    length, width = h1_ref.shape

    @pl.loop(0, GROUPS)
    def _(g):
        cols, feats = tile(g, WIDE), tile(g, SLIM)
        plain, turned = projection_blocks(proj_ref, g)
        weight = w_qkv_ref.at[g]
        shared = nn(hbar_ref[...].astype(BF16), w_qkv_ref[g, :, 2 * WIDE :])[0:1]
        v_span = pl.ds(pl.multiple_of(2 * width + g * WIDE, WIDE), WIDE)

        @pl.loop(0, length // 512)
        def _(r):
            rows = tile(r, 512)
            projected = nn(h1_ref[rows, :], weight[...])
            v_ref[rows, cols] = (projected[:, 2 * WIDE :] - shared).astype(BF16)
            for kind, (feat_ref, slope_ref) in enumerate(((fq_ref, sq_ref), (fk_ref, sk_ref))):
                span = pl.ds(pl.multiple_of(kind * width + g * WIDE, WIDE), WIDE)
                x = projected[:, kind * WIDE : (kind + 1) * WIDE] + vec_ref[BIAS_QKV : BIAS_QKV + 1, span]
                u = nt((x * twice(cos_ref[rows, :])).astype(BF16), plain) + nt(
                    (x * twice(sin_ref[rows, :])).astype(BF16), turned
                )
                small = jnp.exp(-jnp.abs(u))
                feat_ref[rows, feats] = (jnp.maximum(u, 0.0) + jnp.log1p(small)).astype(BF16)
                slope_ref[rows, feats] = jnp.where(u >= 0.0, 1.0, small) / (1.0 + small)
            checkpoint(poll, g, 5, 0, r, 2)

        shared = shared + vec_ref[BIAS_QKV : BIAS_QKV + 1, v_span]
        segment_states(fk_ref, one_ref, v_ref[:, cols], g, state_ref, g * STATE)
        total_ref[:, feats] = nn(one_ref[...], fk_ref[:, feats])
        checkpoint(poll, g, 5, 2)

        @pl.loop(0, length // 512)
        def _(r):
            rows = tile(r, 512)
            fq = fq_ref[rows, feats]
            numerator = nn(spread(fq, ids_ref[rows, :]), state_ref[tile(g, STATE), :])
            _rows, wide, _slim, absent = denominators(fq, one_ref[:, rows], total_ref[:, feats])
            centred = numerator / wide
            attc_ref[rows, cols] = centred.astype(BF16)
            att_ref[rows, cols] = (centred + (1.0 - absent) * shared).astype(BF16)
            checkpoint(poll, g, 5, 3, r, 2)


def phase_middle(tok_ref, att_ref, w_out_ref, vec_ref, mid_ref, h2_ref):
    length, width = tok_ref.shape

    @pl.loop(0, length // 512)
    def _(r):
        rows = tile(r, 512)
        middle = (
            tok_ref[rows, :].astype(F32)
            + nn(att_ref[rows, :], w_out_ref[...])
            + vec_ref[BIAS_OUT : BIAS_OUT + 1, :width]
        )
        mid_ref[rows, :] = middle
        normed, _inv = normalize(middle)
        hidden = normed * vec_ref[GAIN2 : GAIN2 + 1, :width] + vec_ref[SHIFT2 : SHIFT2 + 1, :width]
        h2_ref[rows, :] = hidden.astype(BF16)


def phase_gelu(h2_ref, w_in_ref, vec_ref, act_ref, slope_ref, first, count):
    @pl.loop(0, count)
    def _(j):
        cols = tile(first + j, 256)
        pre = nn(h2_ref[...], w_in_ref[:, cols]) + vec_ref[BIAS_IN : BIAS_IN + 1, cols]
        gate = 0.5 * (1.0 + lax.erf(pre * 0.7071067811865476))
        act_ref[:, cols] = (pre * gate).astype(BF16)
        slope = gate + pre * jnp.exp(-0.5 * pre * pre) * 0.3989422804014327
        slope_ref[:, cols] = slope.astype(BF16)


def phase_output(mid_ref, act_refs, w_ffo_refs, vec_ref, out_ref, poll=None):
    length, width = mid_ref.shape

    @pl.loop(0, length // 512)
    def _(r):
        rows = tile(r, 512)
        total = mid_ref[rows, :] + vec_ref[BIAS_FFO : BIAS_FFO + 1, :width]
        for act_ref, w_ffo_ref in zip(act_refs, w_ffo_refs):
            total = total + nn(act_ref[rows, :], w_ffo_ref[...])
        out_ref[rows, :] = total.astype(BF16)
        checkpoint(poll, r, 1)


def phase_grad_pre(cot_ref, w_ffo_ref, slope_ref, gpre_ref, small_ref, poll=None):
    @pl.loop(0, w_ffo_ref.shape[0] // 256)
    def _(j):
        cols = tile(j, 256)
        grad = nt(cot_ref[...], w_ffo_ref[cols, :]) * slope_ref[:, cols].astype(F32)
        grad = grad.astype(BF16)
        gpre_ref[:, cols] = grad
        small_ref[BIAS_IN : BIAS_IN + 1, cols] = column_sum(grad.astype(F32))
        checkpoint(poll, j, 1)


def phase_ffo_grad(act_ref, cot_ref, g_ffo_ref, first, count):
    @pl.loop(0, count)
    def _(i):
        rows = tile(first + i, 384)
        g_ffo_ref[rows, :] = tn(act_ref[:, rows], cot_ref[...]).astype(BF16)


def phase_in_grad(h2_ref, gpre_ref, out_ref, number, poll=None, first=0):
    width = h2_ref.shape[1]

    @pl.loop(0, width // 384)
    def _(i):
        rows = tile(i, 384)
        out_ref[rows, :] = tn(h2_ref[:, rows], gpre_ref[:, tile(number, width)]).astype(BF16)
        checkpoint(poll, (number - first) * 2 + i)


def phase_weight_grad(left_ref, right_ref, out_ref, poll=None):
    chunk, tall = min(768, right_ref.shape[1]), 384

    @pl.loop(0, right_ref.shape[1] // chunk)
    def _(j):
        cols = tile(j, chunk)

        @pl.loop(0, left_ref.shape[1] // tall)
        def _(i):
            rows = tile(i, tall)
            out_ref[rows, cols] = tn(left_ref[:, rows], right_ref[:, cols]).astype(BF16)
            checkpoint(poll, j * (left_ref.shape[1] // tall) + i)


def phase_norm_two_back(
    gpre_ref, w_in_ref, mid_ref, cot_ref, vec_ref, gmid_ref, gbr_ref, small_ref, poll=None
):
    length, width = mid_ref.shape
    small_ref[GAIN2 : SHIFT2 + 1, :width] = jnp.zeros((2, width), F32)
    small_ref[BIAS_FFO : BIAS_FFO + 1, :width] = jnp.zeros((1, width), F32)
    small_ref[BIAS_OUT : BIAS_OUT + 1, :width] = jnp.zeros((1, width), F32)

    @pl.loop(0, length // 512)
    def _(r):
        rows = tile(r, 512)
        incoming = nt(gpre_ref[rows, :], w_in_ref[...])
        normed, inv_std = normalize(mid_ref[rows, :])
        upstream = cot_ref[rows, :].astype(F32)
        grad = upstream + normalize_back(incoming, normed, inv_std, vec_ref[GAIN2 : GAIN2 + 1, :width])
        gmid_ref[rows, :] = grad
        branch = grad.astype(BF16)
        gbr_ref[rows, :] = branch
        small_ref[GAIN2 : GAIN2 + 1, :width] += column_sum(incoming * normed)
        small_ref[SHIFT2 : SHIFT2 + 1, :width] += column_sum(incoming)
        small_ref[BIAS_FFO : BIAS_FFO + 1, :width] += column_sum(upstream)
        small_ref[BIAS_OUT : BIAS_OUT + 1, :width] += column_sum(branch.astype(F32))
        checkpoint(poll, r, 1)


def phase_attention_back(
    gbr_ref, w_out_ref, attc_ref, proj_ref, cos_ref, sin_ref, one_ref, ids_ref,
    fq_ref, fk_ref, sq_ref, sk_ref, v_ref, state_ref, total_ref,
    dnum_ref, dstate_ref, dtotal_ref, gproj_ref, small_ref, h1_ref, g_qkv_ref, arrive, poll=None,
):
    length, width = gbr_ref.shape

    @pl.loop(0, GROUPS)
    def _(g):
        cols, feats = tile(g, WIDE), tile(g, SLIM)
        q_span = cols
        k_span = pl.ds(pl.multiple_of(width + g * WIDE, WIDE), WIDE)
        v_span = pl.ds(pl.multiple_of(2 * width + g * WIDE, WIDE), WIDE)
        plain, turned = projection_blocks(proj_ref, g)
        q_place, k_place, v_place = (tile(3 * g + kind, WIDE) for kind in range(3))
        dtotal_ref[...] = jnp.zeros_like(dtotal_ref)
        for span in (q_span, k_span, v_span):
            small_ref[BIAS_QKV : BIAS_QKV + 1, span] = jnp.zeros((1, WIDE), F32)

        def unrotate(grad, rows, span, place):
            high, low = split_two(grad)
            back = (nn(high, plain) + nn(low, plain)) * twice(cos_ref[rows, :])
            back = back + (nn(high, turned) + nn(low, turned)) * twice(sin_ref[rows, :])
            back = back.astype(BF16)
            gproj_ref[rows, place] = back
            small_ref[BIAS_QKV : BIAS_QKV + 1, span] += column_sum(back.astype(F32))

        @pl.loop(0, length // 512)
        def _(r):
            rows = tile(r, 512)
            grad_att = nt(gbr_ref[rows, :], w_out_ref[cols, :])
            fq = fq_ref[rows, feats]
            total_rows, wide, slim, _absent = denominators(fq, one_ref[:, rows], total_ref[:, feats])
            dnum = (grad_att / wide).astype(BF16)
            dnum_ref[rows, :] = dnum
            dots = nn(
                (dnum.astype(F32) * attc_ref[rows, cols].astype(F32)).astype(BF16),
                ones_where(head_blocks(WIDE, SLIM, HEAD_DIM, FEATS)),
            )
            dden = -dots
            dfq = masked_sum(nt(dnum, state_ref[tile(g, STATE), :]), ids_ref[rows, :])
            dfq = dfq + dden * total_rows
            dtotal_ref[...] += nn(one_ref[:, rows], (dden * fq.astype(F32)).astype(BF16))
            unrotate(dfq * sq_ref[rows, feats], rows, q_span, q_place)
            checkpoint(poll, g, 6, 0, r, 2)

        segment_states(fq_ref, one_ref, dnum_ref[...], g, dstate_ref, 0)
        pl.when(g == 0)(arrive)

        @pl.loop(0, length // 512)
        def _(r):
            rows = tile(r, 512)
            dv = nn(spread(fk_ref[rows, feats], ids_ref[rows, :]), dstate_ref[...]).astype(BF16)
            gproj_ref[rows, v_place] = dv
            small_ref[BIAS_QKV : BIAS_QKV + 1, v_span] += column_sum(dv.astype(F32))
            high, low = split_two(dtotal_ref[...])
            one_rows = one_ref[:, rows]
            dfk = masked_sum(nt(v_ref[rows, cols], dstate_ref[...]), ids_ref[rows, :])
            dfk = dfk + tn(one_rows, high) + tn(one_rows, low)
            unrotate(dfk * sk_ref[rows, feats], rows, k_span, k_place)
            checkpoint(poll, g, 6, 2, r, 2)

        @pl.loop(0, width // 384)
        def _(i):
            rows = tile(i, 384)
            g_qkv_ref[g, rows, :] = tn(h1_ref[:, rows], gproj_ref[:, tile(g, 3 * WIDE)]).astype(BF16)
            checkpoint(poll, g, 6, 4, i, 2)


def phase_norm_one_back(
    gproj_ref, w_qkv_ref, tok_ref, gmid_ref, vec_ref, tgrad_ref, small_ref, poll=None
):
    length, width = tok_ref.shape
    small_ref[GAIN1 : SHIFT1 + 1, :width] = jnp.zeros((2, width), F32)

    @pl.loop(0, length // 256)
    def _(r):
        rows = tile(r, 256)
        incoming = jnp.zeros((256, width), F32)
        for group in range(GROUPS):
            incoming += nt(gproj_ref[rows, tile(group, 3 * WIDE)], w_qkv_ref[group])
        normed, inv_std = normalize(tok_ref[rows, :].astype(F32))
        back = normalize_back(incoming, normed, inv_std, vec_ref[GAIN1 : GAIN1 + 1, :width])
        tgrad_ref[rows, :] = (gmid_ref[rows, :] + back).astype(BF16)
        small_ref[GAIN1 : GAIN1 + 1, :width] += column_sum(incoming * normed)
        small_ref[SHIFT1 : SHIFT1 + 1, :width] += column_sum(incoming)
        checkpoint(poll, r, 1)


MESH = pl.DeviceIdType.MESH
ORDER = [(d, xr) for xr in (1, 0) for d in (3, 2, 1, 0)]


class Place:
    def __init__(self, depth):
        f, self.y = lax.axis_index("fsdp"), lax.axis_index("dp")
        self.depth = depth
        self.z, self.x, self.c = f // 4, (f // 2) % 2, f % 2

    def index(self, d=0, xr=0, cr=0):
        c = 1 - self.c if cr else self.c
        x = 1 - self.x if xr else self.x
        return ((self.z + d) % self.depth) * 4 + x * 2 + c

    def device(self, d=0, xr=0, cr=0, yr=0):
        return (self.index(d, xr, cr), 1 - self.y if yr else self.y)

    def partners(self):
        far = [self.device(d=d) for d in range(1, self.depth)]
        return far + [self.device(xr=1), self.device(cr=1), self.device(yr=1)]

    def plane(self):
        ways = [(d, xr, cr) for d in range(self.depth) for xr in range(2) for cr in range(2)][1:]
        return [self.device(*way) for way in ways] + [self.device(yr=1)]

    def greet(self, partners=None):
        barrier = pltpu.get_barrier_semaphore()
        partners = self.partners() if partners is None else partners
        for partner in partners:
            pl.semaphore_signal(barrier, inc=1, device_id=partner, device_id_type=MESH)
        pl.semaphore_wait(barrier, len(partners))


class Region:
    def __init__(self, place, ref, stride, base=0, rows=None, columns=None, shared=False):
        self.ref, self.stride, self.base, self.rows = ref, stride, base, stride if rows is None else rows
        start, size = (0, ref.shape[1]) if columns is None else columns
        self.columns, self.width = slice(start, start + size), size
        self.third = third = self.rows // 3
        self.shared, self.all = shared, (0, self.rows)
        if shared:
            self.moved = self.common = self.all
            return
        self.moved = (place.y * third, 2 * third)
        self.mine, self.other = (place.y * 2 * third, third), ((1 - place.y) * 2 * third, third)
        self.common = (third, third)

    def where(self, index, span):
        start, size = span
        return pl.ds(pl.multiple_of(index * self.stride + self.base + start, 16), size), self.columns

    def at(self, index, span):
        return self.ref.at[self.where(index, span)]

    def bulk(self, thirds):
        return self.ref.at[pl.ds(0, thirds * self.third), self.columns]


def remote(src, dst, send, recv, device):
    return pltpu.make_async_remote_copy(
        src_ref=src, dst_ref=dst, send_sem=send, recv_sem=recv, device_id=device, device_id_type=MESH
    )


class Gather:
    def __init__(self, place, full, sems, pieces):
        self.place, self.full, self.sems, self.pieces = place, full, sems, pieces
        depth = place.depth
        self.z, self.x, self.y = 0, depth, 2 * depth
        self.sibling, self.sent, self.own = 4 * depth, 4 * depth + 1, 4 * depth + 2

    @staticmethod
    def count(depth):
        return 4 * depth + 3

    def copy(self, index, span, slot, device):
        ref = self.full.at(index, span)
        return remote(ref, ref, self.sems.at[self.sent], self.sems.at[slot], device)

    def fetch(self):
        for src, dst in self.pieces:
            pltpu.make_async_copy(src, dst, self.sems.at[self.own]).start()

    def start(self):
        place, full = self.place, self.full
        mine = full.at(place.index(), full.all)
        pltpu.make_async_copy(mine, mine, self.sems.at[self.own]).wait()
        for d in (2, 1, 3):
            self.copy(place.index(), full.moved, self.z + d, place.device(d=d)).start()
        self.copy(place.index(), full.moved, self.x, place.device(xr=1)).start()
        self.copy(place.index(), full.all, self.sibling, place.device(cr=1)).start()

    def z_step(self, d):
        place, full = self.place, self.full
        index = place.index(d=place.depth - d)
        self.copy(index, full.moved, self.z + d, place.device()).wait_recv()
        self.copy(index, full.moved, self.x + d, place.device(xr=1)).start()
        self.copy(index, full.mine, self.y + 2 * d, place.device(yr=1)).start()
        self.copy(index, full.moved, self.sibling, place.device(cr=1)).start()

    def x_step(self, d):
        place, full = self.place, self.full
        index = place.index(d=place.depth - d, xr=1)
        self.copy(index, full.moved, self.x + d, place.device()).wait_recv()
        self.copy(index, full.mine, self.y + 2 * d + 1, place.device(yr=1)).start()
        self.copy(index, full.moved, self.sibling, place.device(cr=1)).start()

    def y_step(self, d, xr):
        place, full = self.place, self.full
        index = place.index(d=place.depth - d, xr=xr)
        self.copy(index, full.other, self.y + 2 * d + xr, place.device()).wait_recv()
        self.copy(index, full.other, self.sibling, place.device(cr=1)).start()

    def done(self):
        half = self.full.bulk(6 * self.place.depth)
        pltpu.make_async_copy(half, half, self.sems.at[self.sibling]).wait()

    def drain(self):
        depth = self.place.depth
        sent = self.full.bulk(2 * (depth - 1) + 2 + 3 + 5 * (depth - 1) + 3 * depth + 2 * depth - 1)
        pltpu.make_async_copy(sent, sent, self.sems.at[self.sent]).wait()

    def step(self, code):
        if code == 0:
            self.start()
        elif code < 5:
            self.z_step(code - 1)
        elif code < 9:
            self.x_step(code - 5)
        else:
            self.y_step((code - 9) // 2, (code - 9) % 2)


class Reduce:
    def __init__(self, place, full, bufs, sems, emit, source=None):
        self.place, self.full, self.sems, self.emit = place, full, sems, emit
        self.source = full if source is None else source
        depth = place.depth
        self.c_buf, self.y_buf, self.x_buf, self.z_buf, self.f_send, self.f_recv = bufs
        self.c, self.y, self.x, self.z = 0, 2 * depth, 4 * depth, 5 * depth
        self.f, self.sent = 6 * depth, 6 * depth + 1

    @staticmethod
    def count(depth):
        return 6 * depth + 2

    @staticmethod
    def buffers(depth, rows, columns, shared=False):
        third = rows // 3
        if shared:
            tall = (rows, columns)
            shapes = [(2 * depth, *tall), (1, 16, columns), (depth, *tall), (depth - 1, *tall), tall, tall]
            return [pltpu.VMEM(dims, BF16) for dims in shapes]
        return [
            pltpu.VMEM((2 * depth, rows, columns), BF16),
            pltpu.VMEM((2 * depth, third, columns), BF16),
            pltpu.VMEM((depth, 2 * third, columns), BF16),
            pltpu.VMEM((depth - 1, 2 * third, columns), BF16),
            pltpu.VMEM((rows, columns), BF16),
            pltpu.VMEM((rows, columns), BF16),
        ]

    def copy(self, src, dst, slot, device):
        return remote(src, dst, self.sems.at[self.sent], self.sems.at[slot], device)

    def c_copy(self, d, xr):
        slot = 2 * d + xr
        src = self.source.at(self.place.index(d, xr, 1), self.full.all)
        return self.copy(src, self.c_buf.at[slot], self.c + slot, self.place.device(cr=1))

    def y_copy(self, d, xr):
        slot = 2 * d + xr
        src = self.full.at(self.place.index(d, xr), self.full.other)
        return self.copy(src, self.y_buf.at[slot], self.y + slot, self.place.device(yr=1))

    def x_copy(self, d):
        src = self.full.at(self.place.index(d, 1), self.full.moved)
        return self.copy(src, self.x_buf.at[d], self.x + d, self.place.device(xr=1))

    def z_copy(self, d):
        src = self.full.at(self.place.index(d), self.full.moved)
        return self.copy(src, self.z_buf.at[d - 1], self.z + d, self.place.device(d=d))

    def f_rows(self, span):
        start, size = span
        return pl.ds(start if isinstance(start, int) else pl.multiple_of(start, 16), size)

    def f_copy(self):
        rows = self.f_rows(self.full.moved)
        return self.copy(self.f_send.at[rows], self.f_recv.at[rows], self.f, self.place.device(yr=1))

    def add(self, where, values):
        self.full.ref[where] = self.full.ref[where] + values

    def c_send(self, d, xr):
        self.c_copy(d, xr).start()

    def c_step(self, d, xr):
        self.c_copy(d, xr).wait_recv()
        self.add(self.full.where(self.place.index(d, xr), self.full.all), self.c_buf[2 * d + xr])
        if not self.full.shared:
            self.y_copy(d, xr).start()
        elif xr:
            self.x_copy(d).start()

    def y_step(self, d, xr):
        self.y_copy(d, xr).wait_recv()
        self.add(self.full.where(self.place.index(d, xr), self.full.mine), self.y_buf[2 * d + xr])
        if xr:
            self.x_copy(d).start()

    def x_step(self, d):
        self.x_copy(d).wait_recv()
        self.add(self.full.where(self.place.index(d), self.full.moved), self.x_buf[d])
        if d:
            self.z_copy(d).start()

    def z_step(self):
        total = self.full.ref[self.full.where(self.place.index(), self.full.moved)].astype(F32)
        for d in range(1, self.place.depth):
            self.z_copy(d).wait_recv()
            total = total + self.z_buf[d - 1].astype(F32)
        self.f_send[self.f_rows(self.full.moved), :] = total.astype(BF16)
        self.f_copy().start()

    def f_step(self):
        self.f_copy().wait_recv()
        common = self.f_rows(self.full.common)
        if not self.full.shared:
            mine, other = self.f_rows(self.full.mine), self.f_rows(self.full.other)
            self.emit(self.full.mine, self.f_send[mine, :].astype(F32))
            self.emit(self.full.other, self.f_recv[other, :].astype(F32))
        self.emit(self.full.common, self.f_send[common, :].astype(F32) + self.f_recv[common, :].astype(F32))

    def drain(self):
        depth = self.place.depth
        thirds = 9 * depth + 3 * (depth - 1) + 3 if self.full.shared else 12 * depth
        sent = self.full.bulk(thirds)
        pltpu.make_async_copy(sent, sent, self.sems.at[self.sent]).wait()

    def sends(self):
        return [functools.partial(self.c_send, d, xr) for d, xr in ORDER]

    def step(self, code):
        if code < 8:
            self.c_step(code // 2, code % 2)
        elif code < 16:
            self.y_step((code - 8) // 2, code % 2)
        elif code < 20:
            self.x_step(code - 16)
        elif code == 20:
            self.z_step()
        else:
            self.f_step()


class Exchange:
    def __init__(self, place, full, held, sent, got, sems):
        self.place, self.full, self.held, self.sent, self.got, self.sems = place, full, held, sent, got, sems
        self.ways = [(d, xr, cr) for d in range(place.depth) for xr in range(2) for cr in range(2)][1:]

    def copy(self, d, xr, cr):
        slot = ((self.place.depth - d) % self.place.depth) * 4 + xr * 2 + cr
        src = self.full.at[tile(self.place.index(d, xr, cr), 16)]
        sems = self.sems.at[1]
        return remote(src, self.held.at[slot], self.sems.at[0, slot], sems.at[slot], self.place.device(d, xr, cr))

    def start(self):
        for way in self.ways:
            self.copy(*way).start()

    def last(self):
        sems = self.sems
        return remote(self.sent, self.got, sems.at[0, 0], sems.at[1, 0], self.place.device(yr=1))

    def relay(self):
        total = self.full[tile(self.place.index(), 16), :].astype(F32)
        for way in self.ways:
            self.copy(*way).wait()
        for slot in range(1, self.held.shape[0]):
            total = total + self.held[slot].astype(F32)
        self.sent[...] = total.astype(BF16)
        self.last().start()

    def finish(self, emit):
        self.last().wait()
        emit(self.sent[...].astype(F32) + self.got[...].astype(F32))


class Plan:
    def __init__(self, sections, units):
        self.sections, self.units = iter(sections), units

    def take(self):
        return [functools.partial(self.units[number // 32].step, number % 32) for number in next(self.sections)]

    def takes(self, count):
        return [self.take() for _ in range(count)]

    def run(self):
        run(self.take())


def run(steps):
    for step in steps:
        step()


SMALL_ROWS, SMALL_COLUMNS = 48, 256
SMALL_LAYOUT = (
    (GAIN1, 1, 0, 0), (SHIFT1, 1, 0, 1), (BIAS_OUT, 1, 0, 2), (GAIN2, 1, 0, 3), (SHIFT2, 1, 0, 4),
    (BIAS_QKV, 3, 1, 0), (BIAS_FFO, 1, 1, 3), (BIAS_IN, 4, 2, 0),
)


GRAD_LAYOUT = tuple((name, 0, many, third, place) for name, many, third, place in SMALL_LAYOUT if name != BIAS_QKV)
GRAD_LAYOUT += ((QUERY_KEY, 0, 2, 1, 0), (VALUE, 2, 1, 1, 2))


def small_block(vectors):
    unit = vectors[GAIN1].shape[0]
    flat = jnp.zeros((3 * SMALL_COLUMNS,), BF16)
    for name, many, third, place in SMALL_LAYOUT:
        start, size = third * SMALL_COLUMNS + place * unit, many * unit
        flat = flat + jnp.pad(vectors[name], (start, flat.shape[0] - start - size))
    return jnp.pad(flat.reshape(3, 1, SMALL_COLUMNS), ((0, 0), (0, 15), (0, 0))).reshape(SMALL_ROWS, SMALL_COLUMNS)


def selector(unit, many, offset, groups):
    size = unit * many
    lane = iota((SMALL_COLUMNS, size * groups), 1) % size
    return ones_where(iota((SMALL_COLUMNS, size * groups), 0) == lane + offset * unit)


def owner_mask(size, groups):
    return iota((groups, size * groups), 0) == iota((groups, size * groups), 1) // size


def unpack_small(gathered_ref, vec_ref, groups, unit):
    blocks = gathered_ref[...].astype(F32).reshape(groups, SMALL_ROWS, SMALL_COLUMNS)
    thirds = [jnp.sum(blocks[:, 16 * k : 16 * k + 16], axis=1).astype(BF16) for k in range(3)]
    for name, many, third, offset in SMALL_LAYOUT:
        size = unit * many
        laid = nn(thirds[third], selector(unit, many, offset, groups))
        vec_ref[name : name + 1, : size * groups] = column_sum(jnp.where(owner_mask(size, groups), laid, 0.0))


def pack_small(small_ref, out_ref, groups, unit):
    thirds = [jnp.zeros((groups, SMALL_COLUMNS), F32) for _ in range(3)]
    for name, start, many, third, offset in GRAD_LAYOUT:
        size, row = unit * many, name if name < QUERY_KEY else BIAS_QKV
        row = small_ref[row : row + 1, start * unit * groups : (start + many) * unit * groups]
        spaced = jnp.where(owner_mask(size, groups), row, 0.0).astype(BF16)
        thirds[third] = thirds[third] + nt(spaced, selector(unit, many, offset, groups))
    place = iota((groups, 16, SMALL_COLUMNS), 1)
    laid = jnp.zeros((groups, 16, SMALL_COLUMNS), F32)
    for third, part in enumerate(thirds):
        laid = jnp.where(place == third, part[:, None, :], laid)
    out_ref[...] = laid.reshape(groups * 16, SMALL_COLUMNS).astype(BF16)


class Names:
    def __getattr__(self, name):
        return name


N = Names()
GIVEN, LOAD, FAR, MADE, SPILL, SCRATCH, BARE = range(7)


class Arrays:
    COPIES = 48

    def __init__(self, spec, refs, sems):
        self.hbm, self.spec, self.sems, self.open, self.slots, self.puts = {}, spec, sems, [], {}, []
        for name, ref in refs.items():
            setattr(self, name, ref)

    def copy(self, what):
        name, part, parts, axis = (what, 0, 1, 0) if isinstance(what, str) else what
        hbm, vmem = self.hbm[name], getattr(self, name)
        if parts > 1:
            size = vmem.shape[axis] // parts
            span = pl.ds(part * size, size)
            where = (span,) if axis == 0 else (slice(None), span)
            hbm, vmem = hbm.at[where], vmem.at[where]
        sem = self.sems.at[self.slots.setdefault(what, len(self.slots))]
        assert len(self.slots) <= self.COPIES
        if self.spec[name][0] == LOAD:
            return pltpu.make_async_copy(hbm, vmem, sem)
        return pltpu.make_async_copy(vmem, hbm, sem)

    def load(self, *names):
        for name in names:
            self.copy(name).start()

    def ready(self, *names):
        for name in names:
            self.copy(name).wait()

    def spill(self, *names):
        for name in names:
            self.copy(name).start()
            self.open.append(name)

    def settle(self, *names):
        self.ready(*names)
        self.open = [name for name in self.open if name not in names]

    def put(self, src, dst):
        slot = len(self.slots)
        self.slots[slot] = slot
        copy = pltpu.make_async_copy(src, dst, self.sems.at[slot])
        copy.start()
        self.puts.append(copy)
        return copy

    def fetch(self, src, dst):
        copy = self.put(src, dst)
        self.puts.remove(copy)
        return copy

    def close(self):
        self.ready(*self.open)
        for copy in self.puts:
            copy.wait()


def parts_of(name, parts, axis):
    return [(name, part, parts, axis) for part in range(parts)]


def call(name, body, spec, operands, collective_id=None, flops=0):
    ins = [n for n in spec if spec[n][0] in (GIVEN, LOAD, FAR)]
    outs = [n for n in spec if spec[n][0] in (MADE, SPILL, BARE)]
    moved = [n for n in spec if spec[n][0] in (LOAD, SPILL)]
    tmps = [n for n in spec if spec[n][0] == SCRATCH]
    scratch = [pltpu.VMEM(spec[n][1], spec[n][2]) for n in moved] + [spec[n][1] for n in tmps]
    scratch.append(pltpu.SemaphoreType.DMA((Arrays.COPIES,)))

    def kernel(*refs):
        given, made, inner = refs[: len(ins)], refs[len(ins) : len(ins) + len(outs)], refs[len(ins) + len(outs) :]
        arrays = Arrays(spec, dict(zip(moved + tmps, inner)), inner[-1])
        for names, group in ((ins, given), (outs, made)):
            for n, ref in zip(names, group):
                if n in moved:
                    arrays.hbm[n] = ref
                else:
                    setattr(arrays, n, ref)
        body(arrays)
        arrays.close()

    vmem, anywhere = pl.BlockSpec(memory_space=pltpu.VMEM), pl.BlockSpec(memory_space=pl.ANY)
    results = pl.pallas_call(
        kernel,
        out_shape=[jax.ShapeDtypeStruct(spec[n][1], spec[n][2]) for n in outs],
        in_specs=[vmem if spec[n][0] == GIVEN else anywhere for n in ins],
        out_specs=[vmem if spec[n][0] == MADE else anywhere for n in outs],
        scratch_shapes=scratch,
        compiler_params=pltpu.CompilerParams(
            vmem_limit_bytes=VMEM_LIMIT,
            collective_id=collective_id,
            has_side_effects=collective_id is not None,
        ),
        name=name,
    )(*[operands[n] for n in ins])
    return dict(zip(outs, results))


SHARED_FFO = 0
PLAN_FRONT = (
    (32, 64),
    (389,),
    (5, 388, 387, 37, 386, 69, 394, 10, 399, 392, 4, 397, 391, 390, 42, 395, 3, 74, 2, 96, 400, 15, 398, 396, 8, 36,
     13, 7, 35, 11),
    (6, 34, 101, 128),
    (16, 14, 40, 47),
    (68, 45, 39, 67, 12, 66, 160, 38, 43, 106, 48, 133),
    (46, 72, 79, 77, 100),
    (44, 71, 75, 98, 99, 192),
    (70, 138, 165),
    (80, 104, 111, 132),
    (78, 131),
    (),
    (76, 102, 103, 107, 109, 130, 224),
    (112, 143, 164, 170, 197),
    (136, 141, 163),
    (108, 110, 135, 162, 256),
    (134, 139, 175, 229),
    (),
    (144, 168, 196, 195, 202),
    (142, 167, 171, 173, 194, 288),
    (140, 166, 228, 234, 261),
    (176, 200, 207, 227),
    (174, 199, 205, 226, 320),
    (),
    (172, 198, 203, 239, 293),
    (),
    (208, 206, 232, 231, 235, 237, 258, 260, 259, 266, 352),
    (204, 230, 298),
    (),
    (240, 238, 262, 292, 291, 325),
    (264, 267, 271, 269, 290),
    (),
    (236, 263, 268, 303, 324, 323, 357),
    (272, 296, 295, 301, 322, 330),
    (),
    (270, 294, 299, 328, 335, 356, 355),
    (304, 327, 333, 354, 362),
    (302, 326),
    (331, 300, 336, 360, 367, 423, 359, 365, 421, 419, 417, 422, 420, 334, 418, 416, 455, 453, 358, 363, 451, 449,
     454, 452, 332, 450, 448, 487, 485, 483, 481, 368, 486, 484, 482, 480, 519),
    (517, 515, 513, 366, 518),
    (516, 514, 512, 463, 435, 461, 364, 459, 434, 457, 462),
    (433, 460),
    (458, 456),
    (432, 495),
    (493,),
    (467, 491, 489),
    (466, 494),
    (492,),
    (465, 490, 488),
    (464, 527),
    (525,),
    (499, 523, 521),
    (436, 498, 526),
    (524,),
    (497, 522, 520),
    (496,),
    (531,),
    (468, 530),
    (437,),
    (529,),
    (528,),
    (469, 500),
    (),
    (532, 501, 533),
)
PLAN_BACK = (
    (7, 5, 3, 1, 6, 4, 2, 0, 39),
    (37, 35, 33, 38, 36, 34, 32, 71, 69, 67),
    (65, 70, 68, 66, 64, 103, 101, 99, 97, 102),
    (15, 13, 11, 100, 98, 96),
    (9, 14, 12, 10, 135, 133, 131, 129, 134, 132, 130, 128),
    (8, 19, 18, 47, 45, 43, 41, 46),
    (17, 16, 44, 42, 40, 79),
    (77,),
    (75, 73, 147),
    (78, 76, 74, 72, 146),
    (111, 109, 107, 145, 167, 165, 163, 161, 166, 164, 162, 160),
    (20, 51, 50, 105, 110, 108, 106, 104, 144, 175),
    (49, 48, 173, 171, 169, 174),
    (83, 172),
    (82, 148, 170, 168),
    (21, 81, 80),
    (115, 199, 197, 195, 193, 198, 196, 194, 192),
    (52, 114, 113, 112, 149, 207),
    (84, 179, 178, 205, 203, 201, 206),
    (177, 204, 202),
    (176, 200),
    (53, 211),
    (85, 210, 209, 231, 229, 227, 225, 230),
    (116, 208, 228, 226, 224),
    (239,),
    (237, 235),
    (117, 180, 233, 238, 236, 243),
    (212, 234, 232, 242, 241),
    (181, 240, 213, 244, 245),
)


def front_body(k, groups, linked):
    depth, width = groups // 4, k.tok.shape[1]
    unit = width // groups
    k.load(N.cot)
    if linked:
        place = Place(depth)
        index = place.index()

        def gather(number, full, *pieces):
            own = full.where(index, full.all)
            if len(pieces) == 1:
                targets = [full.ref.at[own]]
            else:
                targets = [full.ref.at[own[0], pl.ds(n * WIDE, WIDE)] for n in range(len(pieces))]
            return Gather(place, full, k.gather_sems.at[number], list(zip(pieces, targets)))

        small = gather(0, Region(place, k.small_all, SMALL_ROWS), k.small_block)
        units = [
            gather(
                1 + g,
                Region(place, k.w_qkv.at[g], unit),
                *(k.qkv_block.at[:, pl.ds(kind * width + g * WIDE, WIDE)] for kind in range(3)),
            )
            for g in range(GROUPS)
        ]
        units.append(gather(4, Region(place, k.w_out, unit), k.out_block))
        for n in range(4):
            full = Region(place, k.w_in, unit, columns=(n * width, width))
            units.append(gather(5 + n, full, k.in_block.at[:, pl.ds(n * width, width)]))
        for n in range(4):
            full = Region(place, k.w_ffo, 4 * unit, n * unit, unit)
            units.append(gather(9 + n, full, k.ffo_block.at[pl.ds(n * unit, unit), :]))
        for one in [small] + units:
            one.fetch()
        place.greet()
        units.append(small)

        def into(base):
            def emit(span, values):
                start, size = span
                k.ffo_grad[pl.ds(pl.multiple_of(base + start, 16), size), :] = values

            return emit

        reduces = []
        for n in range(4):
            bufs = [getattr(k, name) for name in buffer_names((N.ffo, n))]
            full = Region(place, k.g_ffo, 4 * unit, n * unit, unit, shared=n == SHARED_FFO)
            reduces.append(Reduce(place, full, bufs, k.reduce_sems.at[n], into(n * unit)))
        plan = Plan(PLAN_FRONT, units + reduces)
        small.start()
        units[0].start()
        segment_masks(k.seg, k.one, k.ids)
        plan.run()
        phase_normalize(k.tok, k.mid)
        plan.run()
        plan.run()
        small.done()
        unpack_small(k.small_all, k.vec, groups, unit)
        k.spill(N.vec)
        plan.run()
        phase_norm_one(k.mid, k.vec, k.h1, k.hbar)
        plan.run()
        plan.run()
        units[0].done()
        sections = []
        for g in range(GROUPS):
            sections += plan.takes(5)
            if g + 1 < GROUPS:
                sections[-1] = sections[-1] + plan.take() + [units[g + 1].done]
        poll = Poll(*sections)
    else:
        k.load(N.w_qkv, N.w_out, N.w_in, N.w_ffo)
        poll = None
        segment_masks(k.seg, k.one, k.ids)
        phase_normalize(k.tok, k.mid)
        phase_norm_one(k.mid, k.vec, k.h1, k.hbar)
        k.ready(N.w_qkv)
    k.spill(N.h1)
    phase_attention(
        k.h1, k.hbar, k.w_qkv, k.vec, k.proj, k.cos, k.sin, k.one, k.ids,
        k.fq, k.fk, k.sq, k.sk, k.v, k.state, k.total, k.att, k.attc, poll,
    )
    k.spill(N.fq, N.fk, N.sq, N.sk, N.v, N.state, N.total, N.att, N.attc)
    if linked:
        plan.run()
        units[3].done()
    else:
        k.ready(N.w_out, N.w_in)
    h2 = k.h1
    k.settle(N.h1)
    phase_middle(k.tok, k.att, k.w_out, k.vec, k.mid, h2)
    mid_out = k.put(k.mid, k.mid_rows)
    k.ready(N.cot)
    if linked:
        k.spill(N.w_qkv, N.w_out)
        plan.run()
    before = between = after = None
    if linked:
        sections = plan.takes(12)
        before = Poll(*(sections[3 * n] + [units[4 + n].done] for n in range(4)))
        between, after = Poll(*sections[1::3]), Poll(*sections[2::3])

    @pl.loop(0, 4)
    def _(n):
        checkpoint(before, n)
        phase_gelu(h2, k.w_in, k.vec, k.act, k.slope, 3 * n, 3)
        checkpoint(between, n)
        phase_ffo_grad(k.act, k.cot, k.g_ffo, 2 * n, 2)
        checkpoint(after, n)

    k.put(k.act, k.act_rows)
    polls = [None] * 4
    if linked:
        for one in reduces:
            run(one.sends())
        for one in units[8:12]:
            plan.run()
            one.done()
        polls = [Poll(*plan.takes(12)), Poll(*plan.takes(6)), Poll(*plan.takes(2)), Poll(*plan.takes(2))]
        k.settle(N.w_qkv, N.w_out)
        for one in units[:4]:
            one.drain()
        k.put(k.w_ffo, k.w_ffo_all)
    else:
        k.spill(N.g_ffo)
        k.ready(N.w_ffo)
    phase_grad_pre(k.cot, k.w_ffo, k.slope, k.slope, k.small, polls[0])

    @pl.loop(0, GROUPS)
    def _(n):
        phase_in_grad(h2, k.slope, k.w_qkv.at[n], n, polls[1])

    phase_in_grad(h2, k.slope, k.w_out, GROUPS, polls[2], GROUPS)
    for n, block in enumerate([k.w_qkv.at[g] for g in range(GROUPS)] + [k.w_out]):
        k.put(block, k.g_in.at[:, pl.ds(n * width, width)])
    k.settle(N.attc)
    mid_out.wait()
    k.puts.remove(mid_out)
    phase_norm_two_back(k.slope, k.w_in, k.mid, k.cot, k.vec, k.mid, k.attc, k.small, polls[3])
    k.put(k.mid, k.gmid)
    k.put(k.attc, k.gbr)
    if linked:
        plan.run()
        for one in units[4:] + reduces:
            one.drain()


def back_body(k, groups, linked):
    depth, width = groups // 4, k.tok.shape[1]
    unit = width // groups
    first = (N.w_out, N.fq, N.attc, N.total, N.state, N.sq)
    later = (N.v, N.fk, N.sk, N.h1)
    k.load(N.att, N.gbr)
    if linked:
        k.load(N.g_in)
    k.load(*first)
    if linked:
        k.load(*later)
    polls = [None] * 3
    if linked:
        place = Place(depth)

        def into(ref, column=0):
            def emit(span, values):
                start, size = span
                start = start if isinstance(start, int) else pl.multiple_of(start, 16)
                ref[pl.ds(start, size), column : column + values.shape[1]] = values

            return emit

        def into_group(group):
            def emit(span, values):
                for kind in range(3):
                    part = values[:, kind * WIDE : (kind + 1) * WIDE]
                    into(k.qkv_grad, kind * width + group * WIDE)(span, part)

            return emit

        def reducer(number, base, full, emit, source=None):
            bufs = [getattr(k, n) for n in buffer_names(base)]
            return Reduce(place, full, bufs, k.reduce_sems.at[number], emit, source)

        wide = [
            reducer(
                n,
                (N.wide, n),
                Region(place, k.g_in, unit, columns=(n * width, width)),
                into(k.in_grad, n * width),
                Region(place, k.hbm[N.g_in], unit, columns=(n * width, width)),
            )
            for n in range(4)
        ]
        out = reducer(4, N.out, Region(place, k.g_out, unit, shared=True), into(k.out_grad))
        qkv = [
            reducer(5 + g, (N.qkv, g), Region(place, k.g_qkv.at[g], unit), into_group(g)) for g in range(GROUPS)
        ]
        small = Exchange(place, k.small_all, k.small_held, k.small_sent, k.small_got, k.small_sems)

        def emit_small(values):
            k.small_grad[...] = values

        place.greet(place.plane())
        units = wide + [out] + qkv
        plan = Plan(PLAN_BACK, units)
        for one in wide:
            run(one.sends())
        first_steps = plan.take()
        sections = plan.takes(2)
        polls = [Poll(sections[0], sections[1] + out.sends())]
        sections = plan.takes(6 * GROUPS)
        for g in range(GROUPS):
            sections[6 * g + 5] = sections[6 * g + 5] + qkv[g].sends()
        polls += [Poll(*sections), Poll(*plan.takes(4))]
    segment_masks(k.seg, k.one, k.ids)
    k.ready(N.att, N.gbr)
    if linked:
        k.ready(N.g_in)
        run(first_steps)
    phase_weight_grad(k.att, k.gbr, k.g_out, polls[0])
    k.ready(*first)
    if not linked:
        k.load(*later)
    k.load(N.w_qkv, N.tok, N.gmid)
    phase_attention_back(
        k.gbr, k.w_out, k.attc, k.proj, k.cos, k.sin, k.one, k.ids, k.fq, k.fk, k.sq, k.sk, k.v,
        k.state, k.total, k.dnum, k.dstate, k.dtotal, k.gproj, k.small, k.h1, k.g_qkv, lambda: k.ready(*later), polls[1],
    )
    k.ready(N.w_qkv, N.tok, N.gmid)
    acts = (k.att, k.attc, k.v, k.gbr)
    w_ffos = (k.w_out, k.w_qkv.at[0], k.w_qkv.at[1], k.w_qkv.at[2])
    fetched = [k.fetch(k.act_rows.at[:, pl.ds(n * width, width)], acts[n]) for n in range(4)]
    fetched.append(k.fetch(k.w_ffo_all.at[pl.ds(0, width), :], w_ffos[0]))
    phase_norm_one_back(k.gproj, k.w_qkv, k.tok, k.gmid, k.vec, k.tgrad, k.small, polls[2])
    k.spill(N.tgrad)
    fetched += [k.fetch(k.w_ffo_all.at[pl.ds(n * width, width), :], w_ffos[n]) for n in range(1, 4)]
    fetched.append(k.fetch(k.mid_rows, k.gmid))
    if linked:
        for row in (BIAS_OUT, GAIN2, SHIFT2, BIAS_FFO, BIAS_IN):
            k.small[row : row + 1, :] = k.small_two[row : row + 1, :]
        pack_small(k.small, k.small_all, groups, unit)
        small.start()
        plan.run()
        final = Poll(*plan.takes(2))
    else:
        final = None
    for copy in fetched:
        copy.wait()
    phase_output(k.gmid, acts, w_ffos, k.vec, k.tok, final)
    k.put(k.tok, k.output)
    if linked:
        last = plan.take()
        run(last[: len(last) // 2])
        small.relay()
        run(last[len(last) // 2 :])
        small.finish(emit_small)
        for one in units:
            one.drain()
    else:
        k.spill(N.g_out, N.g_qkv)


def buffer_names(base):
    base = base if isinstance(base, str) else base[0] + N.g * (1 + base[1])
    return [base + N.b * (1 + n) for n in range(6)]


def position_tables(length):
    half = HEAD_DIM // 2
    frequency = 10000.0 ** (-np.arange(half, dtype=np.float64) / half)
    angles = np.arange(length, dtype=np.float64)[:, None] * frequency[None, :]
    repeat = SLIM // half
    return (
        np.tile(np.cos(angles), (1, repeat)).astype(np.float32),
        np.tile(np.sin(angles), (1, repeat)).astype(np.float32),
    )


def gather(value):
    return lax.all_gather(value, "fsdp", axis=0, tiled=True)


def by_group(weight):
    width = weight.shape[0]
    return weight.reshape(width, 3, GROUPS, WIDE).transpose(2, 0, 1, 3).reshape(GROUPS, width, 3 * WIDE)


def reduce_full(grad):
    piece = lax.psum_scatter(grad.astype(F32), "fsdp", scatter_dimension=0, tiled=True)
    return lax.psum(piece.astype(BF16), "dp").astype(F32)


class Sizes:
    def __init__(self, length, width, hidden, groups, linked):
        self.length, self.width, self.hidden, self.groups, self.linked = length, width, hidden, groups, linked
        self.depth, self.unit = groups // 4, width // groups
        feats = HEADS * FEATS
        rows_wide, rows_feats = (length, width), (length, feats)
        self.weights = dict(
            w_qkv=(GROUPS, width, 3 * WIDE), w_out=(width, width), w_in=(width, hidden), w_ffo=(hidden, width)
        )
        self.common = dict(
            seg=(GIVEN, (1, length), jnp.int32),
            proj=(GIVEN, (feats, HEAD_DIM), F32),
            cos=(GIVEN, (length, SLIM), F32),
            sin=(GIVEN, (length, SLIM), F32),
        )
        self.masks = dict(
            one=(SCRATCH, pltpu.VMEM((SEGS, length), BF16)), ids=(SCRATCH, pltpu.VMEM((length, SLIM), F32))
        )
        self.saved = dict(
            h1=(rows_wide, BF16), fq=(rows_feats, BF16), fk=(rows_feats, BF16), sq=(rows_feats, F32),
            sk=(rows_feats, F32), v=(rows_wide, BF16), state=((GROUPS * STATE, WIDE), BF16),
            total=((SEGS, feats), F32), att=(rows_wide, BF16), attc=(rows_wide, BF16),
        )
        self.rows = rows_wide


def run_front(z, values):
    weights, wide = z.weights, (z.length, z.hidden)
    spec = dict(tok=(GIVEN, z.rows, BF16), cot=(LOAD, z.rows, BF16), **z.common)
    if z.linked:
        spec.update(small_block=(FAR, (SMALL_ROWS, SMALL_COLUMNS), BF16))
        for n in (N.qkv_block, N.out_block, N.in_block, N.ffo_block):
            spec[n] = (FAR, values[n].shape, BF16)
        spec.update({n: (SPILL, weights[n], BF16) for n in (N.w_qkv, N.w_out)})
        spec.update({n: (SCRATCH, pltpu.VMEM(weights[n], BF16)) for n in (N.w_in, N.w_ffo)})
        spec.update(
            vec=(SPILL, (8, z.hidden), F32), w_ffo_all=(BARE, weights[N.w_ffo], BF16),
            small_all=(SCRATCH, pltpu.VMEM((z.groups * SMALL_ROWS, SMALL_COLUMNS), BF16)),
            gather_sems=(SCRATCH, pltpu.SemaphoreType.DMA((13, Gather.count(z.depth)))),
            ffo_grad=(MADE, (z.hidden // z.groups, z.width), F32),
            g_ffo=(SCRATCH, pltpu.VMEM(weights[N.w_ffo], BF16)),
            reduce_sems=(SCRATCH, pltpu.SemaphoreType.DMA((4, Reduce.count(z.depth)))),
        )
        for number in range(4):
            buffers = Reduce.buffers(z.depth, z.unit, z.width, number == SHARED_FFO)
            spec.update({n: (SCRATCH, buf) for n, buf in zip(buffer_names((N.ffo, number)), buffers)})
    else:
        spec.update({n: (LOAD, dims, BF16) for n, dims in weights.items()})
        spec.update(vec=(GIVEN, (8, z.hidden), F32), g_ffo=(SPILL, weights[N.w_ffo], BF16))
    spec.update({n: (SPILL,) + v for n, v in z.saved.items()})
    spec.update(
        z.masks, hbar=(SCRATCH, pltpu.VMEM((8, z.width), F32)), mid=(SCRATCH, pltpu.VMEM(z.rows, F32)),
        act=(SCRATCH, pltpu.VMEM(wide, BF16)), slope=(SCRATCH, pltpu.VMEM(wide, BF16)),
        mid_rows=(BARE, z.rows, F32), act_rows=(BARE, wide, BF16), g_in=(BARE, weights[N.w_in], BF16),
        gmid=(BARE, z.rows, F32),
        gbr=(BARE, z.rows, BF16), small=(MADE, (8, z.hidden), F32),
    )
    return call(N.front, lambda k: front_body(k, z.groups, z.linked), spec, values, 1 if z.linked else None)


def run_back(z, values):
    width, weights = z.width, z.weights
    spec = dict(vec=(GIVEN, (8, z.hidden), F32), **z.common)
    spec.update({n: (LOAD,) + v for n, v in z.saved.items()})
    spec.update(
        tok=(LOAD, z.rows, BF16), gbr=(LOAD, z.rows, BF16), gmid=(LOAD, z.rows, F32),
        w_qkv=(LOAD, weights[N.w_qkv], BF16), w_out=(LOAD, weights[N.w_out], BF16),
        tgrad=(SPILL, z.rows, BF16), output=(BARE, z.rows, BF16), mid_rows=(FAR, z.rows, F32),
        act_rows=(FAR, (z.length, z.hidden), BF16), w_ffo_all=(FAR, weights[N.w_ffo], BF16),
        dnum=(SCRATCH, pltpu.VMEM((z.length, WIDE), BF16)), dstate=(SCRATCH, pltpu.VMEM((STATE, WIDE), BF16)),
        dtotal=(SCRATCH, pltpu.VMEM((SEGS, SLIM), F32)), gproj=(SCRATCH, pltpu.VMEM((z.length, 3 * width), BF16)),
        **z.masks,
    )
    if z.linked:
        spec.update(
            small=(SCRATCH, pltpu.VMEM((8, z.hidden), F32)), small_two=(GIVEN, (8, z.hidden), F32),
            g_in=(LOAD, weights[N.w_in], BF16), g_out=(SCRATCH, pltpu.VMEM(weights[N.w_out], BF16)),
            g_qkv=(SCRATCH, pltpu.VMEM((GROUPS, width, 3 * WIDE), BF16)),
            small_all=(SCRATCH, pltpu.VMEM((z.groups * 16, SMALL_COLUMNS), BF16)),
            small_held=(SCRATCH, pltpu.VMEM((z.groups, 16, SMALL_COLUMNS), BF16)),
            small_sent=(SCRATCH, pltpu.VMEM((16, SMALL_COLUMNS), BF16)),
            small_got=(SCRATCH, pltpu.VMEM((16, SMALL_COLUMNS), BF16)),
            small_sems=(SCRATCH, pltpu.SemaphoreType.DMA((2, z.groups))),
            in_grad=(MADE, (z.unit, z.hidden), F32), out_grad=(MADE, (z.unit, width), F32),
            qkv_grad=(MADE, (z.unit, 3 * width), F32), small_grad=(MADE, (16, SMALL_COLUMNS), F32),
            reduce_sems=(SCRATCH, pltpu.SemaphoreType.DMA((5 + GROUPS, Reduce.count(z.depth)))),
        )
        names = [N.out] + [(N.wide, n) for n in range(4)] + [(N.qkv, g) for g in range(GROUPS)]
        for base in names:
            buffers = Reduce.buffers(z.depth, z.unit, width, base == N.out)
            spec.update({n: (SCRATCH, buf) for n, buf in zip(buffer_names(base), buffers)})
    else:
        spec.update(
            small=(MADE, (8, z.hidden), F32), g_out=(SPILL, weights[N.w_out], BF16),
            g_qkv=(SPILL, (GROUPS, width, 3 * WIDE), BF16),
        )
    return call(N.back, lambda k: back_body(k, z.groups, z.linked), spec, values, 2 if z.linked else None)


def run_finish(z, values):
    names = (N.output, N.tgrad, N.in_grad, N.ffo_grad, N.qkv_grad, N.out_grad)
    sizes = [z.unit * many for _name, _start, many, _third, _place in GRAD_LAYOUT]

    def kernel(*refs):
        ins, small, refs = refs[: len(names)], refs[len(names)], refs[len(names) + 1 :]
        outs, smalls, refs = refs[: len(names)], refs[len(names) : len(names) + len(sizes)], refs[len(names) + len(sizes) :]
        held, sems = refs[: len(names)], refs[len(names)]
        for n in range(len(names)):
            pltpu.make_async_copy(ins[n], held[n], sems.at[n]).start()
        for (_name, _start, many, third, place), ref in zip(GRAD_LAYOUT, smalls):
            ref[...] = small[third : third + 1, place * z.unit : (place + many) * z.unit]
        for n in range(len(names)):
            pltpu.make_async_copy(ins[n], held[n], sems.at[n]).wait()
            pltpu.make_async_copy(held[n], outs[n], sems.at[n]).start()
        for n in range(len(names)):
            pltpu.make_async_copy(held[n], outs[n], sems.at[n]).wait()

    vmem, anywhere = pl.BlockSpec(memory_space=pltpu.VMEM), pl.BlockSpec(memory_space=pl.ANY)
    arrays = [values[n] for n in names]
    results = pl.pallas_call(
        kernel,
        out_shape=[jax.ShapeDtypeStruct(a.shape, a.dtype) for a in arrays]
        + [jax.ShapeDtypeStruct((1, size), F32) for size in sizes],
        in_specs=[anywhere] * len(names) + [vmem],
        out_specs=[anywhere] * len(names) + [vmem] * len(sizes),
        scratch_shapes=[pltpu.VMEM(a.shape, a.dtype) for a in arrays] + [pltpu.SemaphoreType.DMA((len(names),))],
        compiler_params=pltpu.CompilerParams(vmem_limit_bytes=VMEM_LIMIT),
        name=N.finish,
    )(*arrays, values[N.small_grad])
    smalls = {row[0]: v.reshape(-1) for row, v in zip(GRAD_LAYOUT, results[len(names) :])}
    return dict(zip(names, results)), smalls


def body(
    linked,
    tokens, segment_ids, projection, norm1_gain, norm1_bias, qkv_weight, qkv_bias, out_weight, out_bias,
    norm2_gain, norm2_bias, in_weight, in_bias, ffn_out_weight, ffn_out_bias, cotangent,
):
    length, width = tokens.shape
    hidden = in_weight.shape[1]
    groups = lax.axis_size(N.fsdp)
    z = Sizes(length, width, hidden, groups, linked)
    cos, sin = position_tables(length)
    vectors = {
        GAIN1: norm1_gain, SHIFT1: norm1_bias, BIAS_OUT: out_bias, GAIN2: norm2_gain, SHIFT2: norm2_bias,
        BIAS_FFO: ffn_out_bias, BIAS_QKV: qkv_bias, BIAS_IN: in_bias,
    }
    values = dict(
        tok=tokens, seg=segment_ids, proj=projection.reshape(HEADS * FEATS, HEAD_DIM), cos=cos, sin=sin,
        cot=cotangent, qkv_block=qkv_weight, out_block=out_weight, in_block=in_weight, ffo_block=ffn_out_weight,
    )
    if linked:
        values.update(small_block=small_block(vectors))
    else:
        values.update(
            w_qkv=by_group(gather(qkv_weight)), w_out=gather(out_weight), w_in=gather(in_weight), w_ffo=gather(ffn_out_weight),
            vec=jnp.stack(
                [
                    jnp.pad(gather(vectors[n]).astype(F32), (0, hidden - vectors[n].shape[0] * groups))
                    for n in range(len(vectors))
                ]
            ),
        )
    made = run_front(z, values)
    small_two = made.pop(N.small)
    made.setdefault(N.w_ffo_all, values.get(N.w_ffo))
    values.update(made, small_two=small_two)
    values.update(run_back(z, values))
    if linked:
        made, smalls = run_finish(z, values)
        values.update(made)
        grads = [values[n] for n in (N.qkv_grad, N.out_grad, N.in_grad, N.ffo_grad)]
    else:
        small_one = values[N.small]
        full = {
            n: (small_one if n in (GAIN1, SHIFT1, BIAS_QKV) else small_two)[n, : vectors[n].shape[0] * groups]
            for n in vectors
        }
        smalls = {n: reduce_full(v) for n, v in full.items() if n != BIAS_QKV}
        smalls[QUERY_KEY] = reduce_full(full[BIAS_QKV][: 2 * width])
        smalls[VALUE] = reduce_full(full[BIAS_QKV][2 * width :])
        g_qkv = values[N.g_qkv].reshape(GROUPS, width, 3, WIDE).transpose(1, 2, 0, 3).reshape(width, 3 * width)
        grads = [reduce_full(g) for g in (g_qkv, values[N.g_out], values[N.g_in], values[N.g_ffo])]
    return (
        values[N.output], values[N.tgrad], smalls[GAIN1], smalls[SHIFT1], grads[0], smalls[QUERY_KEY],
        smalls[VALUE], grads[1], smalls[BIAS_OUT], smalls[GAIN2], smalls[SHIFT2], grads[2], smalls[BIAS_IN],
        grads[3], smalls[BIAS_FFO],
    )


def solution(mesh):
    rows = P(("fsdp", "dp"), None)
    vector, matrix = P("fsdp"), P("fsdp", None)
    in_specs = (
        rows, rows, P(), vector, vector, matrix, vector, matrix, vector,
        vector, vector, matrix, vector, matrix, vector, rows,
    )
    out_specs = (
        rows, rows, vector, vector, matrix, vector, vector, matrix, vector,
        vector, vector, matrix, vector, matrix, vector,
    )
    linked = mesh.shape["fsdp"] == 16 and mesh.shape["dp"] == 2
    return jax.shard_map(
        functools.partial(body, linked), mesh=mesh, in_specs=in_specs, out_specs=out_specs, check_vma=False
    )
```

profile of v0, /device:TPU:0, one launch (start us, length us, event | category | flops | bytes accessed | tf_op | source)
XLA Modules:
  0.0 184.0 jit_solution(4890105090300453916)
XLA Ops:
  0.6 0.9 pad_add_fusion
  1.5 0.6 pad.44.clone
  2.1 108.0 %front.1 = (bf16[3,768,768]{2,1,0:T(8,128)(2,1)}, bf16[768,768]{1,0:T(8,128)(2,1)}, f32[8,3072]{1,0:T(8,128)}, bf16[3072,768]{1,0:T(8,128)(2,1)}, f32[192,768]{1...) custom-call(bf16[1024,768]{1,0:T(8,128)(2,1)} %refs_15_.1, ...), custom_call_target="tpu_custom_call" | custom-call | tf_op jit(solution)/shard_map/front/pallas_call | solution.py:884
  110.1 68.7 %back.1 = (bf16[1024,768]{1,0:T(8,128)(2,1)}, bf16[1024,768]{1,0:T(8,128)(2,1)}, f32[48,3072]{1,0:T(8,128)}, f32[48,768]{1,0:T(8,128)}, f32[48,2304]{1,0:T(8,128)}, /*index=5*/f32[16,256]{1,0:T(8,128)}) custom-call(f32[8,3072]{1,0:T(8,128)} %get-tuple-element.57.refs_0_, s32[1,1024]{1,0:T(1,128)} %refs_1_.3, f32[384,64]{1,0:T(8,128)} %bitcast.12, ...), custom_call_target="tpu_custom_call" | custom-call | tf_op jit(solution)/shard_map/back/pallas_call | solution.py:884
  178.8 5.0 %finish.1 = (bf16[1024,768]{1,0:T(8,128)(2,1)}, bf16[1024,768]{1,0:T(8,128)(2,1)}, f32[48,3072]{1,0:T(8,128)}, f32[192,768]{1,0:T(8,128)}, f32[48,2304]{1,0:T(8,...) custom-call(bf16[1024,768]{1,0:T(8,128)(2,1)} %get-tuple-element.77., ...), custom_call_target="tpu_custom_call" | custom-call | tf_op jit(solution)/shard_map/finish/pallas_call | solution.py:1413
  (1 shorter events, 0.0 us)
where the time goes:
time: 184 us
  Pallas kernels  182 us (99%)
    pallas_call x2, Pallas kernels, call(): pl.pallas_call(kernel, out_shape=[jax.ShapeDtypeStruct(spec[n][1], spec[n...  177 us
    pallas_call x1, Pallas kernels, run_finish(): pl.pallas_call(kernel, out_shape=[jax.ShapeDtypeStruct(a.shape, a.dtype)...  5 us

commit v1 on v0

--- a/solution.py
+++ b/solution.py
@@ -1395,18 +1395,30 @@
     sizes = [z.unit * many for _name, _start, many, _third, _place in GRAD_LAYOUT]
 
     def kernel(*refs):
-        ins, small, refs = refs[: len(names)], refs[len(names)], refs[len(names) + 1 :]
+        ins, far, refs = refs[: len(names)], refs[len(names)], refs[len(names) + 1 :]
         outs, smalls, refs = refs[: len(names)], refs[len(names) : len(names) + len(sizes)], refs[len(names) + len(sizes) :]
-        held, sems = refs[: len(names)], refs[len(names)]
+        held, small, sems = refs[: len(names)], refs[len(names)], refs[len(names) + 1]
+
+        def halves(src, dst, n):
+            size = src.shape[0] // 2
+            spans = [pl.ds(part * size, size) for part in range(2)]
+            return [pltpu.make_async_copy(src.at[x], dst.at[x], sems.at[2 * n + p]) for p, x in enumerate(spans)]
+
+        last = pltpu.make_async_copy(far, small, sems.at[2 * len(names)])
+        last.start()
         for n in range(len(names)):
-            pltpu.make_async_copy(ins[n], held[n], sems.at[n]).start()
+            for copy in halves(ins[n], held[n], n):
+                copy.start()
+        last.wait()
         for (_name, _start, many, third, place), ref in zip(GRAD_LAYOUT, smalls):
             ref[...] = small[third : third + 1, place * z.unit : (place + many) * z.unit]
         for n in range(len(names)):
-            pltpu.make_async_copy(ins[n], held[n], sems.at[n]).wait()
-            pltpu.make_async_copy(held[n], outs[n], sems.at[n]).start()
+            for arrived, onward in zip(halves(ins[n], held[n], n), halves(held[n], outs[n], n)):
+                arrived.wait()
+                onward.start()
         for n in range(len(names)):
-            pltpu.make_async_copy(held[n], outs[n], sems.at[n]).wait()
+            for copy in halves(held[n], outs[n], n):
+                copy.wait()
 
     vmem, anywhere = pl.BlockSpec(memory_space=pltpu.VMEM), pl.BlockSpec(memory_space=pl.ANY)
     arrays = [values[n] for n in names]
@@ -1414,9 +1426,10 @@
         kernel,
         out_shape=[jax.ShapeDtypeStruct(a.shape, a.dtype) for a in arrays]
         + [jax.ShapeDtypeStruct((1, size), F32) for size in sizes],
-        in_specs=[anywhere] * len(names) + [vmem],
+        in_specs=[anywhere] * (len(names) + 1),
         out_specs=[anywhere] * len(names) + [vmem] * len(sizes),
-        scratch_shapes=[pltpu.VMEM(a.shape, a.dtype) for a in arrays] + [pltpu.SemaphoreType.DMA((len(names),))],
+        scratch_shapes=[pltpu.VMEM(a.shape, a.dtype) for a in arrays]
+        + [pltpu.VMEM((16, SMALL_COLUMNS), F32), pltpu.SemaphoreType.DMA((2 * len(names) + 1,))],
         compiler_params=pltpu.CompilerParams(vmem_limit_bytes=VMEM_LIMIT),
         name=N.finish,
     )(*arrays, values[N.small_grad])

time: 184 us -> 184 us (level)
  no operation moved by 1% of the time
where the time goes in v1:
time: 184 us; the launch traced here: 183 us
  Pallas kernels  181 us (98%)
    pallas_call x2, Pallas kernels, call(): pl.pallas_call(kernel, out_shape=[jax.ShapeDtypeStruct(spec[n][1], spec[n...  177 us
    pallas_call x1, Pallas kernels, run_finish(): pl.pallas_call(kernel, out_shape=[jax.ShapeDtypeStruct(a.shape, a.dtype)...  4.51 us

profile of v1, /device:TPU:0, one launch (start us, length us, event | category | flops | bytes accessed | tf_op | source)
XLA Modules:
  0.0 183.5 jit_solution(4388440285063927353)
XLA Ops:
  0.6 0.9 pad_add_fusion
  1.5 0.6 pad.44.clone
  2.1 108.0 %front.1 = (bf16[3,768,768]{2,1,0:T(8,128)(2,1)}, bf16[768,768]{1,0:T(8,128)(2,1)}, f32[8,3072]{1,0:T(8,128)}, bf16[3072,768]{1,0:T(8,128)(2,1)}, f32[192,768]{1...) custom-call(bf16[1024,768]{1,0:T(8,128)(2,1)} %refs_15_.1, ...), custom_call_target="tpu_custom_call" | custom-call | tf_op jit(solution)/shard_map/front/pallas_call | solution.py:884
  110.1 68.7 %back.1 = (bf16[1024,768]{1,0:T(8,128)(2,1)}, bf16[1024,768]{1,0:T(8,128)(2,1)}, f32[48,3072]{1,0:T(8,128)}, f32[48,768]{1,0:T(8,128)}, f32[48,2304]{1,0:T(8,128)}, /*index=5*/f32[16,256]{1,0:T(8,128)}) custom-call(f32[8,3072]{1,0:T(8,128)} %get-tuple-element.57.refs_0_, s32[1,1024]{1,0:T(1,128)} %refs_1_.3, f32[384,64]{1,0:T(8,128)} %bitcast.12, ...), custom_call_target="tpu_custom_call" | custom-call | tf_op jit(solution)/shard_map/back/pallas_call | solution.py:884
  178.8 4.5 %finish.1 = (bf16[1024,768]{1,0:T(8,128)(2,1)}, bf16[1024,768]{1,0:T(8,128)(2,1)}, f32[48,3072]{1,0:T(8,128)}, f32[192,768]{1,0:T(8,128)}, f32[48,2304]{1,0:T(8,...) custom-call(bf16[1024,768]{1,0:T(8,128)(2,1)} %get-tuple-element.77., ...), custom_call_target="tpu_custom_call" | custom-call | tf_op jit(solution)/shard_map/finish/pallas_call | solution.py:1425
  (1 shorter events, 0.0 us)
